TPU v7x, 32 devices: a whole 2x2x4 slice. The times are simulated.
32 devices in a mesh: pairs: 8 (over z, y), dom: 4 (over x, core).
Axes of the slice: x: 2, y: 2, z: 4, core: 2. Of those that a mesh axis runs over, the one named last changes fastest.
Arguments:
- amplitude: bfloat16 [64, 384, 384], P('pairs', 'dom'), may hold values from -2 to 2
- integrals: bfloat16 [64, 384, 384], P('pairs', 'dom'), may hold values from -6 to 6
- virtual_energy: float32 [64, 384], P('pairs'), may hold values from 0.2 to 1.5
- occupied_gap: float32 [64], P('pairs'), may hold values from 0.3 to 1.5
- pair_slot: int32 [64], replicated, may hold values from 0 to 63, as said below
- coupling_source: int32 [128], replicated, may hold values from 0 to 63, as said below
- coupling_target: int32 [128], replicated, may hold values from 0 to 63, as said below
- coupling_fock: float32 [128], P(('pairs', 'dom')), may hold values from -3 to 3
- coupling_intersection: bfloat16 [128, 384, 384], P(('pairs', 'dom')), may hold values from -0.3125 to 0.3125
Outputs:
- updated_amplitude: float32 [64, 384, 384], P('pairs', 'dom')
- residual: float32 [64, 384, 384], P('pairs', 'dom')
Inputs may be any that keep to these rules, and one draw needn't show every extreme that they name: A permutation: pair p is stored at position pair_slot[p], which lies on index pair_slot[p] // 8 of pairs. `coupling_target`: coupling c is held by index c // 16 of pairs, and its target pair is stored on that same index; the two couplings that share a source pair on one holder have different targets. `coupling_source`: among the 16 couplings of one holder, every source pair appears in exactly two, and there are 8 distinct source pairs; of the pairs stored on any one index of pairs, a holder uses at most 2 distinct ones as sources, and exactly 2 for some indices on every holder.
All inputs are finite; a program needn't handle non-finite values.
Results may differ from a plain program's by a relative error of at most 0.0024.
Values may be sent and summed in bfloat16 or wider, within the bound.
A program may use at most 128 MiB of HBM per device.

v0:
```python
import jax
import jax.numpy as jnp
from jax import lax
from jax.sharding import PartitionSpec as P

SRC_CAP = 2


def lookup(table, indices):
    places = jnp.arange(table.shape[0], dtype=jnp.int32)
    return jnp.sum(jnp.where(indices[:, None] == places[None, :], table[None, :], 0), axis=1)


def per_device(
    amplitude,
    integrals,
    virtual_energy,
    occupied_gap,
    pair_slot,
    coupling_source,
    coupling_target,
    coupling_fock,
    coupling_intersection,
):
    holders = lax.axis_size("pairs")
    quarters = lax.axis_size("dom")
    own_pair = lax.axis_index("pairs")
    own_quarter = lax.axis_index("dom")
    pair_count, row_count, width = amplitude.shape
    couplings = coupling_source.shape[0] // holders
    quarter_couplings = coupling_intersection.shape[0]
    source_slot = lookup(pair_slot, coupling_source).reshape(holders, couplings)
    target_slot = lookup(pair_slot, coupling_target).reshape(holders, couplings)
    source_owner = source_slot // pair_count
    source_local = source_slot % pair_count
    held_owner = lax.dynamic_index_in_dim(source_owner, own_pair, 0, keepdims=False)
    held_local = lax.dynamic_index_in_dim(source_local, own_pair, 0, keepdims=False)
    held_target = lax.dynamic_index_in_dim(target_slot, own_pair, 0, keepdims=False) % pair_count
    local_numbers = jnp.arange(pair_count, dtype=jnp.int32)
    owner_numbers = jnp.arange(holders, dtype=jnp.int32)
    capacity = SRC_CAP
    wanted = jnp.any(
        (source_owner[:, :, None] == own_pair)
        & (source_local[:, :, None] == local_numbers[None, None, :]),
        axis=1,
    )
    wanted_count = wanted.astype(jnp.int32)
    order = jnp.cumsum(wanted_count, axis=1) - wanted_count
    slot_numbers = jnp.arange(capacity, dtype=jnp.int32)
    chosen = wanted[:, None, :] & (order[:, None, :] == slot_numbers[None, :, None])
    picked = jnp.sum(jnp.where(chosen, local_numbers[None, None, :], 0), axis=2)
    match = (held_owner[:, None, None] == owner_numbers[None, :, None]) & (
        held_local[:, None, None] == local_numbers[None, None, :]
    )
    needed = jnp.any(match, axis=0).astype(jnp.int32)
    held_order = jnp.cumsum(needed, axis=1) - needed
    held_rank = jnp.sum(jnp.where(match, held_order[None], 0), axis=(1, 2))
    held_slot = held_owner * capacity + held_rank
    energy_rows = lax.dynamic_slice_in_dim(virtual_energy, own_quarter * row_count, row_count, 1)
    denominator = energy_rows[:, :, None] + virtual_energy[:, None, :] + occupied_gap[:, None, None]
    target_select = (held_target[None, :] == local_numbers[:, None]).astype(jnp.bfloat16)
    quarter_select = lax.dynamic_slice_in_dim(
        target_select, own_quarter * quarter_couplings, quarter_couplings, 1
    )
    current = amplitude.astype(jnp.float32)
    sent = current.astype(jnp.bfloat16)
    outgoing = jnp.take(sent, picked.reshape(-1), axis=0).reshape(
        holders, capacity, row_count, width
    )
    arrived = lax.all_to_all(outgoing, "pairs", split_axis=0, concat_axis=0, tiled=True)
    held_rows = jnp.take(arrived.reshape(holders * capacity, row_count, width), held_slot, axis=0)
    grouped = held_rows.reshape(quarters, quarter_couplings, row_count, width)
    whole = lax.all_to_all(grouped, "dom", split_axis=0, concat_axis=2, tiled=True).reshape(
        quarter_couplings, quarters * row_count, width
    )
    left = jnp.einsum(
        "cab,cbd->cad", coupling_intersection, whole, preferred_element_type=jnp.float32
    ).astype(jnp.bfloat16)
    projected = jnp.einsum(
        "cad,ced->cae", left, coupling_intersection, preferred_element_type=jnp.float32
    )
    coupled_term = (coupling_fock[:, None, None] * projected).astype(jnp.bfloat16)
    partial_sum = jnp.dot(
        quarter_select,
        coupled_term.reshape(quarter_couplings, -1),
        preferred_element_type=jnp.float32,
    )
    partial_sum = partial_sum.reshape(pair_count, quarters * row_count, width)
    coupled = lax.psum_scatter(partial_sum, "dom", scatter_dimension=1, tiled=True)
    residual = integrals.astype(jnp.float32) + denominator * current - coupled
    current = current - residual / denominator
    return (current, residual)


def solution(mesh):
    in_specs = (
        P("pairs", "dom", None),
        P("pairs", "dom", None),
        P("pairs", None),
        P("pairs"),
        P(),
        P(),
        P(),
        P(("pairs", "dom")),
        P(("pairs", "dom"), None, None),
    )
    out_specs = (P("pairs", "dom", None), P("pairs", "dom", None))
    return jax.shard_map(
        per_device, mesh=mesh, in_specs=in_specs, out_specs=out_specs, check_vma=False
    )
```

profile of v0, /device:TPU:1, one launch (start us, length us, event | category | flops | bytes accessed | tf_op | source)
XLA Modules:
  0.0 132.1 jit_solution(11512935350733123053)
XLA Ops:
  7.2 0.0 copy-start
  7.2 0.9 select_reduce_fusion.1
  8.1 0.1 reshape.242
  8.2 0.2 fusion.5
  8.4 0.2 reduce_window_sum.18
  8.6 0.2 select_reduce_fusion.2
  8.7 0.1 copy.34
  8.8 0.1 reshape.243
  8.9 0.1 copy.33
  9.0 1.9 %gather_fusion = bf16[16,96,384]{2,1,0:T(8,128)(2,1)S(1)} fusion(bf16[8,96,384]{2,1,0:T(8,128)(2,1)} %param.9, s32[1024]{0:T(1024)S(1)} %pad_clamp_fusion.1), kind=kCustom, calls=%fused_computation | custom fusion | bytes 2359360 | tf_op jit(solution)/shard_map/jit(_take)/gather | solution.py:67
  10.9 1.2 broadcast_select_fusion
  12.1 6.4 %all-to-all-start = ((bf16[8,2,96,384]{3,2,1,0:T(8,128)(2,1)}), bf16[8,2,96,384]{3,2,1,0:T(8,128)(2,1)S(1)}, u32[]{:S(2)}, u32[]{:S(2)}) async-start(bf16[8,2,96,384]{3,2,1,0:T(8,128)(2,1)} %broadcast_select_fusion), calls=%async_computation | async-start | bytes 2359296 | tf_op jit(solution)/shard_map/all_to_all | solution.py:70
  18.5 0.1 reshape.241
  18.6 0.2 and_reduce_fusion
  18.9 0.2 reduce_window_sum.17
  19.0 0.1 fusion.3
  19.1 0.1 reduce_sum.43
  19.2 0.1 mul.41
  19.3 26.9 %all-to-all-done = bf16[8,2,96,384]{3,2,1,0:T(8,128)(2,1)S(1)} async-done(((bf16[8,2,96,384]{3,2,1,0:T(8,128)(2,1)}), bf16[8,2,96,384]{3,2,1,0:T(8,128)(2,1)S(1)}, u32[]{:S(2)}, u32[]{:S(2)}) %all-to-all-start) | async-done | bytes 1179680 | tf_op jit(solution)/shard_map/all_to_all | solution.py:70
  46.2 0.8 gather_fusion.1
  47.1 1.2 broadcast_select_fusion.1
  48.3 5.3 %all-to-all-start.1 = ((bf16[4,4,96,384]{3,2,1,0:T(8,128)(2,1)}), bf16[4,4,96,384]{3,2,1,0:T(8,128)(2,1)S(1)}, u32[]{:S(2)}, u32[]{:S(2)}) async-start(bf16[4,4,96,384]{3,2,1,0:T(8,128)(2,1)} %broadcast_select_fusion.1), calls=%async_computation.1 | async-start | bytes 2359296 | tf_op jit(solution)/shard_map/all_to_all | solution.py:73
  53.5 0.0 reduce-scatter.2.cloned.1.call-start
  53.5 0.1 dynamic-slice
  53.6 14.8 %all-to-all-done.1 = bf16[4,4,96,384]{3,2,1,0:T(8,128)(2,1)S(1)} async-done(((bf16[4,4,96,384]{3,2,1,0:T(8,128)(2,1)}), bf16[4,4,96,384]{3,2,1,0:T(8,128)(2,1)S(1)}, u32[]{:S(2)}, u32[]{:S(2)}) %all-to-all-start.1) | async-done | bytes 1179680 | tf_op jit(solution)/shard_map/all_to_all | solution.py:73
  68.4 0.0 copy-start.5
  68.4 0.1 copy.35
  68.6 0.0 copy-done
  68.6 0.5 copy-done.5
  69.1 1.8 %fusion = bf16[1,4,384,384]{3,2,1,0:T(8,128)(2,1)S(1)} fusion(bf16[4,384,384]{2,1,0:T(8,128)(2,1)S(1)} %copy-done, bf16[4,384,384]{2,1,0:T(8,128)(2,1)S(1)} %bitcast.42, f32[4]{0:T(128)S(1)} %copy-done.5), kind=kOutput, calls=%fused_computation.6 | convolution fusion | flops 907739136 | bytes 3538960 | tf_op jit(solution)/shard_map/cad,ced->cae/dot_general | solution.py:79
  70.9 3.7 %fusion.10 = f32[8,384,384]{2,0,1:T(8,128)} fusion(s32[4]{0:T(128)S(1)} %dynamic-slice, bf16[1,4,384,384]{3,2,1,0:T(8,128)(2,1)S(1)} %fusion), kind=kOutput, calls=%fused_computation.46 | convolution fusion | flops 9437216 | bytes 5898256 | tf_op jit(solution)/shard_map/dot_general | solution.py:83
  74.6 0.0 copy-start.3
  74.6 0.0 copy-start.1
  74.6 0.0 copy-start.2
  74.6 0.0 copy-start.4
  74.6 0.0 reduce-scatter.2.cloned.1.call-update
  74.6 0.7 copy-done.3
  75.3 0.1 constant_dynamic-slice_fusion.3
  75.3 0.1 copy.32
  75.4 45.5 %reduce-scatter.2.cloned.1.call-done = f32[8,96,384]{2,0,1:T(8,128)} async-done(((f32[8,384,384]{2,0,1:T(8,128)}), f32[8,96,384]{2,0,1:T(8,128)}) %reduce-scatter.2.cloned.1.call-update) | async-done | bytes 1179664 | tf_op jit(solution)/shard_map/reduce_scatter | solution.py:89
  121.0 0.0 copy-done.1
  121.0 0.0 copy-done.2
  121.0 0.0 copy-done.4
  121.0 1.8 %convert_subtract_fusion = (f32[8,96,384]{2,0,1:T(8,128)S(1)}, f32[8,96,384]{2,0,1:T(8,128)S(1)}) fusion(f32[8]{0:T(128)S(1)} %copy-done.4, f32[8,384]{1,0:T(8,128)S(1)} %copy-done.3, f32[8,96]{0,1:T(8,128)S(1)} %copy.32, bf16[8,96,384]{2,1,0:T(8,128)(2,1)S(1)} %copy-done.1, f32[8,96,384]{2,0,1:T(8,128)} %reduce-scatter.2.cloned.1.call-done, ...), kind=kLoop, calls=%fused_computation.4 | loop fusion | flops 2654208 | bytes 4733984 | tf_op jit(solution)/shard_map/sub | solution.py:91
  122.8 1.2 copy.38
  124.0 1.2 copy.39
  (16 shorter events, 0.1 us)
Async XLA Ops:
  7.2 61.4 %copy-start = (bf16[4,384,384]{2,1,0:T(8,128)(2,1)S(1)}, bf16[4,384,384]{2,1,0:T(8,128)(2,1)}, u32[]{:S(2)}) copy-start(bf16[4,384,384]{2,1,0:T(8,128)(2,1)} %param.17) | copy-start | bytes 3538948
  12.1 34.1 %all-to-all-start = ((bf16[8,2,96,384]{3,2,1,0:T(8,128)(2,1)}), bf16[8,2,96,384]{3,2,1,0:T(8,128)(2,1)S(1)}, u32[]{:S(2)}, u32[]{:S(2)}) async-start(bf16[8,2,96,384]{3,2,1,0:T(8,128)(2,1)} %broadcast_select_fusion), calls=%async_computation | async-start | bytes 2359296 | tf_op jit(solution)/shard_map/all_to_all | solution.py:70
  48.3 20.1 %all-to-all-start.1 = ((bf16[4,4,96,384]{3,2,1,0:T(8,128)(2,1)}), bf16[4,4,96,384]{3,2,1,0:T(8,128)(2,1)S(1)}, u32[]{:S(2)}, u32[]{:S(2)}) async-start(bf16[4,4,96,384]{3,2,1,0:T(8,128)(2,1)} %broadcast_select_fusion.1), calls=%async_computation.1 | async-start | bytes 2359296 | tf_op jit(solution)/shard_map/all_to_all | solution.py:73
  53.5 67.4 %reduce-scatter.2.cloned.1.call-start = ((), (), s32[]{:S(2)}) async-start(), calls=%async_computation.3 | async-start | bytes 5898240 | tf_op jit(solution)/shard_map/reduce_scatter | solution.py:89
  68.4 0.7 copy-start.5
  74.6 0.7 copy-start.3
  74.6 46.4 %copy-start.1 = (bf16[8,96,384]{2,1,0:T(8,128)(2,1)S(1)}, bf16[8,96,384]{2,1,0:T(8,128)(2,1)}, u32[]{:S(2)}) copy-start(bf16[8,96,384]{2,1,0:T(8,128)(2,1)} %param.9) | copy-start | bytes 1769476
  74.6 46.4 %copy-start.2 = (bf16[8,96,384]{2,1,0:T(8,128)(2,1)S(1)}, bf16[8,96,384]{2,1,0:T(8,128)(2,1)}, u32[]{:S(2)}) copy-start(bf16[8,96,384]{2,1,0:T(8,128)(2,1)} %param.10) | copy-start | bytes 1769476
  74.6 46.4 %copy-start.4 = (f32[8]{0:T(128)S(1)}, f32[8]{0:T(128)}, u32[]{:S(2)}) copy-start(f32[8]{0:T(128)} %param.12) | copy-start | bytes 100
Sparse Core Ops, SparseCore 0:
  74.7 46.2 reduce-scatter.1
where the time goes:
time: 133 us; the launch traced here: 132 us
  waiting for transfers between devices  87.3 us (66%)
  between operations  14.2 us (11%)
  starting transfers between devices  11.6 us (9%)
  local copies, waits for them, and re-layouts  7.28 us (5%)
  other arithmetic  6.27 us (5%)
  matrix products  5.49 us (4%)
    reduce_scatter x1, waiting for transfers between devices, per_device(): lax.psum_scatter(partial_sum, 'dom', scatter_dimension=1, tiled=True)  45.5 us
    all_to_all x1, waiting for transfers between devices, per_device(): lax.all_to_all(outgoing, 'pairs', split_axis=0, concat_axis=0, tiled=True)  26.9 us
    all_to_all x1, waiting for transfers between devices, per_device(): lax.all_to_all(grouped, 'dom', split_axis=0, concat_axis=2, tiled=True)  14.8 us
    all_to_all x1, starting transfers between devices, per_device(): lax.all_to_all(outgoing, 'pairs', split_axis=0, concat_axis=0, tiled=True)  6.37 us
    all_to_all x1, starting transfers between devices, per_device(): lax.all_to_all(grouped, 'dom', split_axis=0, concat_axis=2, tiled=True)  5.26 us
    dot_general x1, matrix products, per_device(): jnp.dot(quarter_select, coupled_term.reshape(quarter_couplings, -1), pref...  3.69 us
    unnamed x14, local copies, waits for them, and re-layouts  3.64 us
  transfers between devices with their start and end apart: 3, of which 3 were waited for; matrix products, arithmetic and copies ran while one was open for 1% of the time, Pallas kernels for 0%

commit v1 on v0

--- a/solution.py
+++ b/solution.py
@@ -59,9 +59,6 @@
     energy_rows = lax.dynamic_slice_in_dim(virtual_energy, own_quarter * row_count, row_count, 1)
     denominator = energy_rows[:, :, None] + virtual_energy[:, None, :] + occupied_gap[:, None, None]
     target_select = (held_target[None, :] == local_numbers[:, None]).astype(jnp.bfloat16)
-    quarter_select = lax.dynamic_slice_in_dim(
-        target_select, own_quarter * quarter_couplings, quarter_couplings, 1
-    )
     current = amplitude.astype(jnp.float32)
     sent = current.astype(jnp.bfloat16)
     outgoing = jnp.take(sent, picked.reshape(-1), axis=0).reshape(
@@ -80,13 +77,16 @@
         "cad,ced->cae", left, coupling_intersection, preferred_element_type=jnp.float32
     )
     coupled_term = (coupling_fock[:, None, None] * projected).astype(jnp.bfloat16)
-    partial_sum = jnp.dot(
-        quarter_select,
-        coupled_term.reshape(quarter_couplings, -1),
-        preferred_element_type=jnp.float32,
+    scattered = lax.all_to_all(
+        coupled_term.reshape(quarter_couplings, quarters, row_count, width),
+        "dom",
+        split_axis=1,
+        concat_axis=0,
+        tiled=True,
+    ).reshape(couplings, row_count, width)
+    coupled = jnp.einsum(
+        "pc,crd->prd", target_select, scattered, preferred_element_type=jnp.float32
     )
-    partial_sum = partial_sum.reshape(pair_count, quarters * row_count, width)
-    coupled = lax.psum_scatter(partial_sum, "dom", scatter_dimension=1, tiled=True)
     residual = integrals.astype(jnp.float32) + denominator * current - coupled
     current = current - residual / denominator
     return (current, residual)

time: 133 us -> 89 us (0.67)
  waiting for transfers between devices: 87.3 us -> 41.6 us
  blocking collectives: 0 us -> 19.1 us
  between operations: 14.2 us -> 0.76 us
  other arithmetic: 6.27 us -> 3.46 us
  matrix products: 5.49 us -> 3.99 us
    reduce_scatter x1 -> x0, waiting for transfers between devices: 45.5 us -> none  [per_device(): lax.psum_scatter(partial_sum, 'dom', scatter_dimension=1, tiled=True)]
    all_to_all x0 -> x1, blocking collectives: none -> 19.1 us  [per_device(): lax.all_to_all(grouped, 'dom', split_axis=0, concat_axis=2, tiled=True)]
    sub x1 -> x0, other arithmetic: 1.8 us -> none  [per_device(): current = current - residual / denominator]
    dot_general x1, matrix products: 3.69 us -> 2.16 us  [per_device(): jnp.einsum('pc,crd->prd', target_select, scattered, preferred_element_typ...]
    unnamed x14 -> x12, local copies, waits for them, and re-layouts: 3.64 us -> 2.97 us
  transfers between devices with their start and end apart: 3 -> 2, of which waited for: 3 -> 2; matrix products, arithmetic and copies ran while one was open for 1% -> 1% of each run, Pallas kernels for 0% -> 0%
where the time goes in v1:
time: 89 us; the launch traced here: 87.7 us
  waiting for transfers between devices  41.6 us (47%)
  blocking collectives  19.1 us (21%)
  starting transfers between devices  11 us (12%)
  local copies, waits for them, and re-layouts  7.69 us (9%)
  matrix products  3.99 us (4%)
  other arithmetic  3.46 us (4%)
    all_to_all x1, waiting for transfers between devices, per_device(): lax.all_to_all(outgoing, 'pairs', split_axis=0, concat_axis=0, tiled=True)  27 us
    all_to_all x1, blocking collectives, per_device(): lax.all_to_all(grouped, 'dom', split_axis=0, concat_axis=2, tiled=True)  19.1 us
    all_to_all x1, waiting for transfers between devices, per_device(): lax.all_to_all(coupled_term.reshape(quarter_couplings, quarters, row_coun...  14.6 us
    all_to_all x1, starting transfers between devices, per_device(): lax.all_to_all(outgoing, 'pairs', split_axis=0, concat_axis=0, tiled=True)  6.37 us
    all_to_all x1, starting transfers between devices, per_device(): lax.all_to_all(coupled_term.reshape(quarter_couplings, quarters, row_coun...  4.67 us
    unnamed x12, local copies, waits for them, and re-layouts  2.97 us
    dot_general x1, matrix products, per_device(): jnp.einsum('pc,crd->prd', target_select, scattered, preferred_element_typ...  2.16 us
    gather x1, local copies, waits for them, and re-layouts, per_device(): jnp.take(sent, picked.reshape(-1), axis=0)  1.87 us
  transfers between devices with their start and end apart: 2, of which 2 were waited for; matrix products, arithmetic and copies ran while one was open for 1% of the time, Pallas kernels for 0%

profile of v1, /device:TPU:1, one launch (start us, length us, event | category | flops | bytes accessed | tf_op | source)
XLA Modules:
  0.0 87.7 jit_solution(5788474851340077103)
XLA Ops:
  0.6 0.0 copy-start
  0.7 0.9 select_reduce_fusion.1
  1.5 0.1 reshape.244
  1.6 0.2 fusion.4
  1.9 0.2 reduce_window_sum.18
  2.0 0.2 select_reduce_fusion.2
  2.2 0.1 copy.47
  2.3 0.1 copy.46
  2.4 0.1 reshape.245
  2.5 1.9 %gather_fusion = bf16[16,96,384]{2,1,0:T(8,128)(2,1)S(1)} fusion(bf16[8,96,384]{2,1,0:T(8,128)(2,1)} %param.9, s32[1024]{0:T(1024)S(1)} %pad_clamp_fusion.1), kind=kCustom, calls=%fused_computation | custom fusion | bytes 2359360 | tf_op jit(solution)/shard_map/jit(_take)/gather | solution.py:64
  4.4 1.2 %broadcast_select_fusion = bf16[8,2,96,384]{3,2,1,0:T(8,128)(2,1)} fusion(bf16[8,2,96,384]{3,2,1,0:T(8,128)(2,1)S(1)} %bitcast.39, pred[8,2]{1,0:T(8,128)(4,1)S(1)} %copy.46), kind=kLoop, calls=%fused_computation.10 | loop fusion | flops 589824 | bytes 2359312 | tf_op jit(solution)/shard_map/jit(_take)/select_n | solution.py:64
  5.6 6.4 %all-to-all-start = ((bf16[8,2,96,384]{3,2,1,0:T(8,128)(2,1)}), bf16[8,2,96,384]{3,2,1,0:T(8,128)(2,1)S(1)}, u32[]{:S(2)}, u32[]{:S(2)}) async-start(bf16[8,2,96,384]{3,2,1,0:T(8,128)(2,1)} %broadcast_select_fusion), calls=%async_computation | async-start | bytes 2359296 | tf_op jit(solution)/shard_map/all_to_all | solution.py:67
  12.0 0.1 mul.37
  12.1 0.2 and_reduce_fusion
  12.3 0.2 reduce_window_sum.17
  12.5 0.1 fusion.2
  12.6 0.1 reduce_sum.43
  12.7 27.0 %all-to-all-done = bf16[8,2,96,384]{3,2,1,0:T(8,128)(2,1)S(1)} async-done(((bf16[8,2,96,384]{3,2,1,0:T(8,128)(2,1)}), bf16[8,2,96,384]{3,2,1,0:T(8,128)(2,1)S(1)}, u32[]{:S(2)}, u32[]{:S(2)}) %all-to-all-start) | async-done | bytes 1179680 | tf_op jit(solution)/shard_map/all_to_all | solution.py:67
  39.7 0.8 gather_fusion.1
  40.5 0.2 broadcast_select_fusion.1
  40.7 19.1 %all_to_all.35 = bf16[4,4,96,384]{3,2,1,0:T(8,128)(2,1)S(1)} all-to-all(bf16[4,4,96,384]{3,2,1,0:T(8,128)(2,1)S(1)} %broadcast_select_fusion.1), channel_id=1, replica_groups=mesh['pairs'=8,'dom'=4] {'dom'}, dimensions={0} | all-to-all | bytes 2359296 | tf_op jit(solution)/shard_map/all_to_all | solution.py:70
  59.9 0.0 copy-start.3
  59.9 0.1 copy.48
  60.0 0.0 copy-done
  60.0 0.5 copy-done.3
  60.5 1.8 %multiply_convert_fusion = bf16[4,384,384]{2,1,0:T(8,128)(2,1)S(1)} fusion(bf16[4,384,384]{2,1,0:T(8,128)(2,1)S(1)} %copy-done, bf16[4,384,384]{2,1,0:T(8,128)(2,1)S(1)} %bitcast.42, f32[4]{0:T(128)S(1)} %copy-done.3), kind=kOutput, calls=%fused_computation.2 | convolution fusion | flops 907739136 | bytes 3538960 | tf_op jit(solution)/shard_map/cad,ced->cae/dot_general | solution.py:76
  62.3 1.2 %copy.51 = bf16[4,4,96,384]{3,2,0,1:T(8,128)(2,1)} copy(bf16[4,4,96,384]{3,2,1,0:T(8,128)(2,1)S(1)} %bitcast.43) | data formatting | bytes 2359296 | tf_op jit(solution)/shard_map/reshape | solution.py:81
  63.5 0.0 copy-start.2
  63.5 0.0 copy-start.1
  63.5 0.0 copy-start.4
  63.5 4.7 %all-to-all-start.2 = ((bf16[4,4,96,384]{3,2,0,1:T(8,128)(2,1)}), bf16[4,4,96,384]{3,2,0,1:T(8,128)(2,1)S(1)}, u32[]{:S(2)}, u32[]{:S(2)}) async-start(bf16[4,4,96,384]{3,2,0,1:T(8,128)(2,1)} %copy.51), calls=%async_computation.2 | async-start | bytes 2359296 | tf_op jit(solution)/shard_map/all_to_all | solution.py:80
  68.2 0.1 reshape.243
  68.3 0.0 copy-done.2
  68.3 0.1 constant_dynamic-slice_fusion.3
  68.3 0.1 copy.45
  68.4 14.6 %all-to-all-done.2 = bf16[4,4,96,384]{3,2,0,1:T(8,128)(2,1)S(1)} async-done(((bf16[4,4,96,384]{3,2,0,1:T(8,128)(2,1)}), bf16[4,4,96,384]{3,2,0,1:T(8,128)(2,1)S(1)}, u32[]{:S(2)}, u32[]{:S(2)}) %all-to-all-start.2) | async-done | bytes 1179680 | tf_op jit(solution)/shard_map/all_to_all | solution.py:80
  83.0 0.0 copy-done.1
  83.1 0.0 copy-done.4
  83.1 2.2 %convert_subtract_fusion = (f32[8,96,384]{2,0,1:T(8,128)S(1)}, f32[8,96,384]{2,0,1:T(8,128)S(1)}) fusion(f32[8]{0:T(128)S(1)} %copy-done.4, f32[8,384]{1,0:T(8,128)S(1)} %copy-done.2, f32[8,96]{0,1:T(8,128)S(1)} %copy.45, bf16[8,96,384]{2,1,0:T(8,128)(2,1)S(1)} %copy-done.1, bf16[16,96,384]{2,1,0:T(8,128)(2,1)S(1)} %bitcast.41, s32[16]{0:T(128)S(1)} %fusion.12, ...), kind=kOutput, calls=%fused_computation.4 | convolution fusion | flops 12091520 | bytes 4734048 | tf_op jit(solution)/shard_map/pc,crd->prd/dot_general | solution.py:87
  85.2 1.2 %copy.53 = f32[8,96,384]{2,1,0:T(8,128)} copy(f32[8,96,384]{2,0,1:T(8,128)S(1)} %get-tuple-element.18) | data formatting | bytes 2359296
  86.4 1.2 %copy.54 = f32[8,96,384]{2,1,0:T(8,128)} copy(f32[8,96,384]{2,0,1:T(8,128)S(1)} %get-tuple-element.19) | data formatting | bytes 2359296
  (16 shorter events, 0.2 us)
Async XLA Ops:
  0.6 59.4 %copy-start = (bf16[4,384,384]{2,1,0:T(8,128)(2,1)S(1)}, bf16[4,384,384]{2,1,0:T(8,128)(2,1)}, u32[]{:S(2)}) copy-start(bf16[4,384,384]{2,1,0:T(8,128)(2,1)} %param.17) | copy-start | bytes 3538948
  5.6 34.1 %all-to-all-start = ((bf16[8,2,96,384]{3,2,1,0:T(8,128)(2,1)}), bf16[8,2,96,384]{3,2,1,0:T(8,128)(2,1)S(1)}, u32[]{:S(2)}, u32[]{:S(2)}) async-start(bf16[8,2,96,384]{3,2,1,0:T(8,128)(2,1)} %broadcast_select_fusion), calls=%async_computation | async-start | bytes 2359296 | tf_op jit(solution)/shard_map/all_to_all | solution.py:67
  59.9 0.7 copy-start.3
  63.5 4.8 %copy-start.2 = (f32[8,384]{1,0:T(8,128)S(1)}, f32[8,384]{1,0:T(8,128)}, u32[]{:S(2)}) copy-start(f32[8,384]{1,0:T(8,128)} %param.11) | copy-start | bytes 36868
  63.5 19.5 %copy-start.1 = (bf16[8,96,384]{2,1,0:T(8,128)(2,1)S(1)}, bf16[8,96,384]{2,1,0:T(8,128)(2,1)}, u32[]{:S(2)}) copy-start(bf16[8,96,384]{2,1,0:T(8,128)(2,1)} %param.9) | copy-start | bytes 1769476
  63.5 19.6 %copy-start.4 = (f32[8]{0:T(128)S(1)}, f32[8]{0:T(128)}, u32[]{:S(2)}) copy-start(f32[8]{0:T(128)} %param.12) | copy-start | bytes 100
  63.5 19.5 %all-to-all-start.2 = ((bf16[4,4,96,384]{3,2,0,1:T(8,128)(2,1)}), bf16[4,4,96,384]{3,2,0,1:T(8,128)(2,1)S(1)}, u32[]{:S(2)}, u32[]{:S(2)}) async-start(bf16[4,4,96,384]{3,2,0,1:T(8,128)(2,1)} %copy.51), calls=%async_computation.2 | async-start | bytes 2359296 | tf_op jit(solution)/shard_map/all_to_all | solution.py:80

commit v2 on v1

v2 whole, which is shorter than its diff:
```python
import functools

import jax
import jax.numpy as jnp
from jax import lax
from jax.experimental import pallas as pl
from jax.experimental.pallas import tpu as pltpu
from jax.sharding import PartitionSpec as P

SRC_CAP = 2
CHUNKS = 2
MESH = pl.DeviceIdType.MESH
VMEM = pltpu.VMEM
SMEM = pltpu.SMEM


def prepare_kernel(
    holders, slot_ref, source_ref, target_ref, amp_ref, out_ref, held_ref, local_ref, first_ref
):
    me = lax.axis_index("pairs")
    pair_count = amp_ref.shape[0]
    couplings = source_ref.shape[0] // holders
    base = me * pair_count
    unroll = 8 if couplings % 8 == 0 else 1

    def holder_step(h, carry):
        def block(i, ab):
            first, second = ab
            for u in range(unroll):
                local = slot_ref[source_ref[h * couplings + i * unroll + u]] - base
                mine = (local >= 0) & (local < pair_count)
                free = first < 0
                second = jnp.where(mine & jnp.logical_not(free) & (local != first), local, second)
                first = jnp.where(mine & free, local, first)
            return first, second

        first, second = lax.fori_loop(
            0, couplings // unroll, block, (jnp.int32(-1), jnp.int32(-1))
        )
        out_ref[h * SRC_CAP] = amp_ref[jnp.maximum(first, 0)]
        out_ref[h * SRC_CAP + 1] = amp_ref[jnp.maximum(second, 0)]
        return carry

    lax.fori_loop(0, holders, holder_step, 0)

    def clear(i, carry):
        first_ref[i] = jnp.int32(-1)
        return carry

    lax.fori_loop(0, holders, clear, 0)

    def own_step(c, carry):
        slot = slot_ref[source_ref[me * couplings + c]]
        owner = lax.div(slot, jnp.int32(pair_count))
        local = slot - owner * pair_count
        known = first_ref[owner]
        first_ref[owner] = jnp.where(known < 0, local, known)
        rank = jnp.where((known < 0) | (known == local), 0, 1)
        held_ref[c] = owner * SRC_CAP + rank
        local_ref[c] = slot_ref[target_ref[me * couplings + c]] - base
        return carry

    lax.fori_loop(0, couplings, own_step, 0)


def exchange_kernel(
    holders,
    quarters,
    held_ref,
    fock_ref,
    out_ref,
    inter_ref,
    terms_ref,
    whole,
    picked,
    sent_terms,
    send1,
    recv1,
    local1,
    send2,
    recv2,
    send3,
    recv3,
    local3,
    *arrived,
):
    me = lax.axis_index("pairs")
    quarter = lax.axis_index("dom")
    chunks = len(arrived)
    slots, chunk_rows, width = arrived[0].shape
    rows = chunk_rows * chunks
    group = inter_ref.shape[0]
    half = holders // 2
    my_half = me // half
    in_half = me % half

    barrier = pltpu.get_barrier_semaphore()

    def greet(j, carry):
        pl.semaphore_signal(
            barrier, inc=1, device_id=((me + j) % holders, quarter), device_id_type=MESH
        )
        return carry

    lax.fori_loop(1, holders, greet, 0)
    for d in range(1, quarters):
        pl.semaphore_signal(
            barrier, inc=1, device_id=(me, (quarter + d) % quarters), device_id_type=MESH
        )
    pl.semaphore_wait(barrier, holders - 1 + quarters - 1)

    def owner_copy(k, h):
        span = pl.ds(k * chunk_rows, chunk_rows)
        return pltpu.make_async_remote_copy(
            src_ref=out_ref.at[pl.ds(h * SRC_CAP, SRC_CAP), span],
            dst_ref=arrived[k].at[pl.ds(me * SRC_CAP, SRC_CAP)],
            send_sem=send1.at[k, h],
            recv_sem=recv1.at[k, me],
            device_id=(h, quarter),
            device_id_type=MESH,
        )

    def arrival(k, h):
        span = pl.ds(k * chunk_rows, chunk_rows)
        return pltpu.make_async_remote_copy(
            src_ref=out_ref.at[pl.ds(h * SRC_CAP, SRC_CAP), span],
            dst_ref=arrived[k].at[pl.ds(h * SRC_CAP, SRC_CAP)],
            send_sem=send1.at[k, h],
            recv_sem=recv1.at[k, h],
            device_id=(h, quarter),
            device_id_type=MESH,
        )

    def own_copy(k):
        span = pl.ds(k * chunk_rows, chunk_rows)
        return pltpu.make_async_copy(
            out_ref.at[pl.ds(me * SRC_CAP, SRC_CAP), span],
            arrived[k].at[pl.ds(me * SRC_CAP, SRC_CAP)],
            local1.at[k],
        )

    for k in range(chunks):

        def far(j, carry, k=k):
            owner_copy(k, (1 - my_half) * half + (in_half + j) % half).start()
            return carry

        def near(j, carry, k=k):
            owner_copy(k, my_half * half + (in_half + j) % half).start()
            return carry

        lax.fori_loop(0, half, far, 0)
        lax.fori_loop(1, half, near, 0)
        own_copy(k).start()

    def peer_copy(k, d):
        peer = (quarter + d) % quarters
        return pltpu.make_async_remote_copy(
            src_ref=picked.at[d - 1, k],
            dst_ref=whole.at[:, pl.ds(pl.multiple_of(quarter * rows + k * chunk_rows, 16), chunk_rows)],
            send_sem=send2.at[k, d],
            recv_sem=recv2.at[k, d],
            device_id=(me, peer),
            device_id_type=MESH,
        )

    def peer_arrival(k, d):
        peer = (quarter + quarters - d) % quarters
        return pltpu.make_async_remote_copy(
            src_ref=picked.at[d - 1, k],
            dst_ref=whole.at[:, pl.ds(pl.multiple_of(peer * rows + k * chunk_rows, 16), chunk_rows)],
            send_sem=send2.at[k, d],
            recv_sem=recv2.at[k, d],
            device_id=(me, peer),
            device_id_type=MESH,
        )

    for k in range(chunks):

        def take(j, carry, k=k):
            arrival(k, (me + j) % holders).wait_recv()
            return carry

        lax.fori_loop(1, holders, take, 0)
        own_copy(k).wait()
        for d in range(1, quarters):
            peer = (quarter + d) % quarters

            def pick(c, carry, k=k, d=d, peer=peer):
                picked[d - 1, k, c] = arrived[k][held_ref[peer * group + c]]
                return carry

            lax.fori_loop(0, group, pick, 0)

        for d in range(1, quarters):
            peer_copy(k, d).start()

        def keep(c, carry, k=k):
            start = pl.multiple_of(quarter * rows + k * chunk_rows, 16)
            whole[c, pl.ds(start, chunk_rows)] = arrived[k][held_ref[quarter * group + c]]
            return carry

        lax.fori_loop(0, group, keep, 0)

    for k in range(chunks):
        for d in range(1, quarters):
            peer_arrival(k, d).wait_recv()

    def term_copy(c, d):
        peer = (quarter + d) % quarters
        return pltpu.make_async_remote_copy(
            src_ref=sent_terms.at[c, pl.ds(pl.multiple_of(peer * rows, 16), rows)],
            dst_ref=terms_ref.at[quarter * group + c],
            send_sem=send3.at[c, d],
            recv_sem=recv3.at[c, d],
            device_id=(me, peer),
            device_id_type=MESH,
        )

    def term_arrival(c, d):
        peer = (quarter + quarters - d) % quarters
        return pltpu.make_async_remote_copy(
            src_ref=sent_terms.at[c, pl.ds(pl.multiple_of(peer * rows, 16), rows)],
            dst_ref=terms_ref.at[peer * group + c],
            send_sem=send3.at[c, d],
            recv_sem=recv3.at[c, d],
            device_id=(me, peer),
            device_id_type=MESH,
        )

    def own_term(c):
        return pltpu.make_async_copy(
            sent_terms.at[c, pl.ds(pl.multiple_of(quarter * rows, 16), rows)],
            terms_ref.at[quarter * group + c],
            local3.at[c],
        )

    def multiply(c, carry):
        inter = inter_ref[c]
        left = jnp.dot(inter, whole[c], preferred_element_type=jnp.float32).astype(jnp.bfloat16)
        projected = lax.dot_general(
            left, inter, (((1,), (1,)), ((), ())), preferred_element_type=jnp.float32
        )
        sent_terms[c] = (fock_ref[c] * projected).astype(jnp.bfloat16)
        for d in range(1, quarters):
            term_copy(c, d).start()
        own_term(c).start()
        return carry

    lax.fori_loop(0, group, multiply, 0)

    def finish(c, carry):
        for d in range(1, quarters):
            term_arrival(c, d).wait_recv()
        for d in range(1, quarters):
            term_copy(c, d).wait_send()
        own_term(c).wait()
        return carry

    lax.fori_loop(0, group, finish, 0)
    for k in range(chunks):

        def sent(j, carry, k=k):
            owner_copy(k, (me + j) % holders).wait_send()
            return carry

        lax.fori_loop(1, holders, sent, 0)
        for d in range(1, quarters):
            peer_copy(k, d).wait_send()


def update_kernel(
    local_ref, gap_ref, terms_ref, amp_ref, integrals_ref, rows_ref, energy_ref, new_ref, residual_ref
):
    p = pl.program_id(0)
    couplings = terms_ref.shape[0]
    residual_ref[0] = jnp.zeros_like(residual_ref[0])
    for c in range(couplings):

        @pl.when(local_ref[c] == p)
        def _():
            residual_ref[0] += terms_ref[c].astype(jnp.float32)

    current = amp_ref[0].astype(jnp.float32)
    denominator = rows_ref[0] + energy_ref[0] + gap_ref[p]
    residual = integrals_ref[0].astype(jnp.float32) + denominator * current - residual_ref[0]
    residual_ref[0] = residual
    new_ref[0] = current - residual / denominator


def per_device(
    amplitude,
    integrals,
    virtual_energy,
    occupied_gap,
    pair_slot,
    coupling_source,
    coupling_target,
    coupling_fock,
    coupling_intersection,
):
    holders = lax.axis_size("pairs")
    quarters = lax.axis_size("dom")
    own_quarter = lax.axis_index("dom")
    pair_count, rows, width = amplitude.shape
    couplings = coupling_source.shape[0] // holders
    group = coupling_intersection.shape[0]
    slots = holders * SRC_CAP
    chunks = CHUNKS
    chunk_rows = rows // chunks
    bf16 = jnp.bfloat16
    in_vmem = pl.BlockSpec(memory_space=VMEM)
    in_smem = pl.BlockSpec(memory_space=SMEM)
    anywhere = pl.BlockSpec(memory_space=pl.ANY)

    outgoing, held, local = pl.pallas_call(
        functools.partial(prepare_kernel, holders),
        out_shape=(
            jax.ShapeDtypeStruct((slots, rows, width), bf16),
            jax.ShapeDtypeStruct((couplings,), jnp.int32),
            jax.ShapeDtypeStruct((couplings,), jnp.int32),
        ),
        in_specs=[in_smem, in_smem, in_smem, in_vmem],
        out_specs=(in_vmem, in_smem, in_smem),
        scratch_shapes=[SMEM((holders,), jnp.int32)],
        name="prepare",
    )(pair_slot, coupling_source, coupling_target, amplitude)

    dma = pltpu.SemaphoreType.DMA
    terms = pl.pallas_call(
        functools.partial(exchange_kernel, holders, quarters),
        out_shape=jax.ShapeDtypeStruct((couplings, rows, width), bf16),
        in_specs=[in_smem, in_smem, anywhere, in_vmem],
        out_specs=anywhere,
        scratch_shapes=[
            VMEM((group, quarters * rows, width), bf16),
            VMEM((quarters - 1, chunks, group, chunk_rows, width), bf16),
            VMEM((group, quarters * rows, width), bf16),
            dma((chunks, holders)),
            dma((chunks, holders)),
            dma((chunks,)),
            dma((chunks, quarters)),
            dma((chunks, quarters)),
            dma((group, quarters)),
            dma((group, quarters)),
            dma((group,)),
        ]
        + [VMEM((slots, chunk_rows, width), bf16)] * chunks,
        compiler_params=pltpu.CompilerParams(
            collective_id=0, has_side_effects=True, vmem_limit_bytes=60 << 20
        ),
        name="exchange",
    )(held, coupling_fock, outgoing, coupling_intersection)

    energy_rows = lax.dynamic_slice_in_dim(virtual_energy, own_quarter * rows, rows, 1)
    block = pl.BlockSpec((1, rows, width), lambda p, *_: (p, 0, 0))
    return pl.pallas_call(
        update_kernel,
        out_shape=(
            jax.ShapeDtypeStruct((pair_count, rows, width), jnp.float32),
            jax.ShapeDtypeStruct((pair_count, rows, width), jnp.float32),
        ),
        grid_spec=pltpu.PrefetchScalarGridSpec(
            num_scalar_prefetch=2,
            grid=(pair_count,),
            in_specs=[
                pl.BlockSpec(
                    (couplings, rows, width), lambda p, *_: (0, 0, 0), pipeline_mode=pl.Buffered(1)
                ),
                block,
                block,
                pl.BlockSpec((1, rows, 1), lambda p, *_: (p, 0, 0)),
                pl.BlockSpec((1, 1, width), lambda p, *_: (p, 0, 0)),
            ],
            out_specs=(block, block),
        ),
        name="update",
    )(
        local,
        occupied_gap,
        terms,
        amplitude,
        integrals,
        energy_rows[:, :, None],
        virtual_energy[:, None, :],
    )


def solution(mesh):
    in_specs = (
        P("pairs", "dom", None),
        P("pairs", "dom", None),
        P("pairs", None),
        P("pairs"),
        P(),
        P(),
        P(),
        P(("pairs", "dom")),
        P(("pairs", "dom"), None, None),
    )
    out_specs = (P("pairs", "dom", None), P("pairs", "dom", None))
    return jax.shard_map(
        per_device, mesh=mesh, in_specs=in_specs, out_specs=out_specs, check_vma=False
    )
```

time: 89 us -> 71.7 us (0.81)
  Pallas kernels: 0 us -> 67.4 us
  waiting for transfers between devices: 41.6 us -> 0 us
  blocking collectives: 19.1 us -> 0 us
  starting transfers between devices: 11 us -> 0 us
  local copies, waits for them, and re-layouts: 7.69 us -> 3.05 us
  matrix products: 3.99 us -> 0 us
  other arithmetic: 3.46 us -> 0 us
    pallas_call x0 -> x3, Pallas kernels: none -> 67.4 us  [the longest x1 56.4 us: per_device(): pl.pallas_call(functools.partial(exchange_kernel, holders, quarters), out...]
    all_to_all x2 -> x0, waiting for transfers between devices: 41.6 us -> none  [the longest x1 27 us: per_device(): lax.all_to_all(outgoing, 'pairs', split_axis=0, concat_axis=0, tiled=True)]
    all_to_all x1 -> x0, blocking collectives: 19.1 us -> none  [per_device(): lax.all_to_all(grouped, 'dom', split_axis=0, concat_axis=2, tiled=True)]
    all_to_all x2 -> x0, starting transfers between devices: 11 us -> none  [the longest x1 6.37 us: per_device(): lax.all_to_all(outgoing, 'pairs', split_axis=0, concat_axis=0, tiled=True)]
    dot_general x2 -> x0, matrix products: 3.99 us -> none  [the longest x1 2.16 us: per_device(): jnp.einsum('pc,crd->prd', target_select, scattered, preferred_element_typ...]
    broadcast_in_dim x0 -> x3, local copies, waits for them, and re-layouts: none -> 3.05 us  [the longest x2 1.74 us: per_device(): energy_rows[:, :, None]]
    unnamed x12 -> x0, local copies, waits for them, and re-layouts: 2.97 us -> none
    gather x2 -> x0, local copies, waits for them, and re-layouts: 2.67 us -> none  [the longest x1 1.87 us: per_device(): jnp.take(sent, picked.reshape(-1), axis=0)]
  transfers between devices with their start and end apart: 2 -> 0, of which waited for: 2 -> 0; matrix products, arithmetic and copies ran while one was open for 1% -> 0% of each run, Pallas kernels for 0% -> 0%
where the time goes in v2:
time: 71.7 us; the launch traced here: 71.1 us
  Pallas kernels  67.4 us (94%)
  local copies, waits for them, and re-layouts  3.05 us (4%)
    pallas_call x1, Pallas kernels, per_device(): pl.pallas_call(functools.partial(exchange_kernel, holders, quarters), out...  56.4 us
    pallas_call x1, Pallas kernels, per_device(): pl.pallas_call(update_kernel, out_shape=(jax.ShapeDtypeStruct((pair_count...  7.71 us
    pallas_call x1, Pallas kernels, per_device(): pl.pallas_call(functools.partial(prepare_kernel, holders), out_shape=(jax...  3.24 us
    broadcast_in_dim x2, local copies, waits for them, and re-layouts, per_device(): energy_rows[:, :, None]  1.74 us

profile of v2, /device:TPU:1, one launch (start us, length us, event | category | flops | bytes accessed | tf_op | source)
XLA Modules:
  0.0 71.1 jit_solution(16038658134630378502)
XLA Ops:
  0.6 0.8 %dynamic-slice_bitcast_fusion = f32[8,96,1]{1,0,2:T(8,128)S(1)} fusion(f32[8,384]{1,0:T(8,128)} %param.11, s32[]{:T(128)S(6)} %select_n.3), kind=kLoop, calls=%fused_computation | loop fusion | bytes 6148 | tf_op jit(solution)/shard_map/broadcast_in_dim | solution.py:384
  1.4 1.3 %broadcast_in_dim.7.energy_ref = f32[8,1,384]{2,1,0:T(1,128)} reshape(f32[8,384]{1,0:T(8,128)} %param.11) | data formatting | bytes 24576 | tf_op jit(solution)/shard_map/broadcast_in_dim | solution.py:385
  2.7 1.0 %copy.11.rows_ref = f32[8,96,1]{2,1,0:T(8,128)} copy(f32[8,96,1]{1,0,2:T(8,128)S(1)} %dynamic-slice_bitcast_fusion) | data formatting | bytes 6144 | tf_op jit(solution)/shard_map/broadcast_in_dim | solution.py:384
  3.7 3.2 %prepare.1 = (bf16[16,96,384]{2,1,0:T(8,128)(2,1)}, s32[16]{0:T(128)}, s32[16]{0:T(128)}) custom-call(s32[64]{0:T(128)} %slot_ref.1, s32[128]{0:T(128)} %source_ref.1, s32[128]{0:T(128)} %target_ref.1, bf16[8,96,384]{2,1,0:T(8,128)(2,1)} %amp_ref.3), custom_call_target="tpu_custom_call" | custom-call | tf_op jit(solution)/shard_map/prepare/pallas_call | solution.py:316
  6.9 56.4 %exchange.1.terms_ref = bf16[16,96,384]{2,1,0:T(8,128)(2,1)} custom-call(s32[16]{0:T(128)} %get-tuple-element.6.held_ref, f32[4]{0:T(128)} %fock_ref.1, bf16[16,96,384]{2,1,0:T(8,128)(2,1)} %get-tuple-element.7.out_ref, bf16[4,384,384]{2,1,0:T(8,128)(2,1)} %inter_ref.1), custom_call_target="tpu_custom_call" | custom-call | tf_op jit(solution)/shard_map/exchange/pallas_call | solution.py:330
  63.4 7.7 %update.1 = (f32[8,96,384]{2,1,0:T(8,128)}, f32[8,96,384]{2,1,0:T(8,128)}) custom-call(s32[16]{0:T(128)} %get-tuple-element.5.local_ref, f32[8]{0:T(128)} %gap_ref.1, bf16[16,96,384]{2,1,0:T(8,128)(2,1)} %exchange.1.terms_ref, bf16[8,96,384]{2,1,0:T(8,128)(2,1)} %amp_ref.3, bf16[8,96,384]{2,1,0:T(8,128)(2,1)} %integrals_ref.1, f32[8,96,1]{2,1,0:T(8,128)} %copy.11.rows_ref, ...), custom_call_target="tpu_custom_call" | custom-call | tf_op jit(solution)/shard_map/update/pallas_call | solution.py:357

commit v3 on v2

--- a/solution.py
+++ b/solution.py
@@ -8,7 +8,7 @@
 from jax.sharding import PartitionSpec as P
 
 SRC_CAP = 2
-CHUNKS = 2
+CHUNK_ROWS = 16
 MESH = pl.DeviceIdType.MESH
 VMEM = pltpu.VMEM
 SMEM = pltpu.SMEM
@@ -270,22 +270,75 @@
 
 
 def update_kernel(
-    local_ref, gap_ref, terms_ref, amp_ref, integrals_ref, rows_ref, energy_ref, new_ref, residual_ref
+    local_ref,
+    gap_ref,
+    terms_hbm,
+    amp_hbm,
+    integrals_hbm,
+    energy_ref,
+    new_hbm,
+    residual_hbm,
+    terms,
+    amp,
+    integrals,
+    new,
+    residual,
+    columns,
+    term_sem,
+    in_sem,
+    out_sem,
 ):
-    p = pl.program_id(0)
-    couplings = terms_ref.shape[0]
-    residual_ref[0] = jnp.zeros_like(residual_ref[0])
-    for c in range(couplings):
-
-        @pl.when(local_ref[c] == p)
-        def _():
-            residual_ref[0] += terms_ref[c].astype(jnp.float32)
-
-    current = amp_ref[0].astype(jnp.float32)
-    denominator = rows_ref[0] + energy_ref[0] + gap_ref[p]
-    residual = integrals_ref[0].astype(jnp.float32) + denominator * current - residual_ref[0]
-    residual_ref[0] = residual
-    new_ref[0] = current - residual / denominator
+    quarter = lax.axis_index("dom")
+    couplings = terms.shape[0]
+    pair_count, rows, width = amp.shape
+
+    def term_copy(c):
+        return pltpu.make_async_copy(terms_hbm.at[c], terms.at[c], term_sem.at[c])
+
+    def in_copies(p):
+        return (
+            pltpu.make_async_copy(amp_hbm.at[p], amp.at[p], in_sem.at[0, p]),
+            pltpu.make_async_copy(integrals_hbm.at[p], integrals.at[p], in_sem.at[1, p]),
+        )
+
+    def out_copies(p):
+        return (
+            pltpu.make_async_copy(new.at[p], new_hbm.at[p], out_sem.at[0, p]),
+            pltpu.make_async_copy(residual.at[p], residual_hbm.at[p], out_sem.at[1, p]),
+        )
+
+    def start_term(c, carry):
+        term_copy(c).start()
+        return carry
+
+    lax.fori_loop(0, couplings, start_term, 0)
+    for p in range(pair_count):
+        for copy in in_copies(p):
+            copy.start()
+    columns[...] = jnp.transpose(energy_ref[...])
+    residual[...] = jnp.zeros_like(residual)
+
+    def add_term(c, carry):
+        term_copy(c).wait()
+        p = local_ref[c]
+        residual[p] = residual[p] + terms[c].astype(jnp.float32)
+        return carry
+
+    lax.fori_loop(0, couplings, add_term, 0)
+    own_rows = columns[pl.ds(pl.multiple_of(quarter * rows, 8), rows), :]
+    for p in range(pair_count):
+        for copy in in_copies(p):
+            copy.wait()
+        current = amp[p].astype(jnp.float32)
+        denominator = own_rows[:, p : p + 1] + energy_ref[p : p + 1, :] + gap_ref[p]
+        rest = integrals[p].astype(jnp.float32) + denominator * current - residual[p]
+        residual[p] = rest
+        new[p] = current - rest / denominator
+        for copy in out_copies(p):
+            copy.start()
+    for p in range(pair_count):
+        for copy in out_copies(p):
+            copy.wait()
 
 
 def per_device(
@@ -306,8 +359,8 @@
     couplings = coupling_source.shape[0] // holders
     group = coupling_intersection.shape[0]
     slots = holders * SRC_CAP
-    chunks = CHUNKS
-    chunk_rows = rows // chunks
+    chunk_rows = CHUNK_ROWS if rows % CHUNK_ROWS == 0 else rows
+    chunks = rows // chunk_rows
     bf16 = jnp.bfloat16
     in_vmem = pl.BlockSpec(memory_space=VMEM)
     in_smem = pl.BlockSpec(memory_space=SMEM)
@@ -352,38 +405,25 @@
         name="exchange",
     )(held, coupling_fock, outgoing, coupling_intersection)
 
-    energy_rows = lax.dynamic_slice_in_dim(virtual_energy, own_quarter * rows, rows, 1)
-    block = pl.BlockSpec((1, rows, width), lambda p, *_: (p, 0, 0))
+    out = jax.ShapeDtypeStruct((pair_count, rows, width), jnp.float32)
     return pl.pallas_call(
         update_kernel,
-        out_shape=(
-            jax.ShapeDtypeStruct((pair_count, rows, width), jnp.float32),
-            jax.ShapeDtypeStruct((pair_count, rows, width), jnp.float32),
-        ),
-        grid_spec=pltpu.PrefetchScalarGridSpec(
-            num_scalar_prefetch=2,
-            grid=(pair_count,),
-            in_specs=[
-                pl.BlockSpec(
-                    (couplings, rows, width), lambda p, *_: (0, 0, 0), pipeline_mode=pl.Buffered(1)
-                ),
-                block,
-                block,
-                pl.BlockSpec((1, rows, 1), lambda p, *_: (p, 0, 0)),
-                pl.BlockSpec((1, 1, width), lambda p, *_: (p, 0, 0)),
-            ],
-            out_specs=(block, block),
-        ),
+        out_shape=(out, out),
+        in_specs=[in_smem, in_smem, anywhere, anywhere, anywhere, in_vmem],
+        out_specs=(anywhere, anywhere),
+        scratch_shapes=[
+            VMEM((couplings, rows, width), bf16),
+            VMEM((pair_count, rows, width), bf16),
+            VMEM((pair_count, rows, width), bf16),
+            VMEM((pair_count, rows, width), jnp.float32),
+            VMEM((pair_count, rows, width), jnp.float32),
+            VMEM((width, pair_count), jnp.float32),
+            dma((couplings,)),
+            dma((2, pair_count)),
+            dma((2, pair_count)),
+        ],
         name="update",
-    )(
-        local,
-        occupied_gap,
-        terms,
-        amplitude,
-        integrals,
-        energy_rows[:, :, None],
-        virtual_energy[:, None, :],
-    )
+    )(local, occupied_gap, terms, amplitude, integrals, virtual_energy)
 
 
 def solution(mesh):

time: 71.7 us -> 63.5 us (0.89)
  Pallas kernels: 67.4 us -> 62.6 us
  local copies, waits for them, and re-layouts: 3.05 us -> 0 us
    pallas_call x1, Pallas kernels: 7.71 us -> 4.19 us  [per_device(): pl.pallas_call(update_kernel, out_shape=(out, out), in_specs=[in_smem, in...]
    broadcast_in_dim x3 -> x0, local copies, waits for them, and re-layouts: 3.05 us -> none  [the longest x2 1.74 us: per_device(): energy_rows[:, :, None]]
    pallas_call x1, Pallas kernels: 56.4 us -> 55.1 us  [per_device(): pl.pallas_call(functools.partial(exchange_kernel, holders, quarters), out...]
where the time goes in v3:
time: 63.5 us; the launch traced here: 63.2 us
  Pallas kernels  62.6 us (99%)
  between operations  0.65 us (1%)
    pallas_call x1, Pallas kernels, per_device(): pl.pallas_call(functools.partial(exchange_kernel, holders, quarters), out...  55.1 us
    pallas_call x1, Pallas kernels, per_device(): pl.pallas_call(update_kernel, out_shape=(out, out), in_specs=[in_smem, in...  4.19 us
    pallas_call x1, Pallas kernels, per_device(): pl.pallas_call(functools.partial(prepare_kernel, holders), out_shape=(jax...  3.25 us

profile of v3, /device:TPU:1, one launch (start us, length us, event | category | flops | bytes accessed | tf_op | source)
XLA Modules:
  0.0 63.2 jit_solution(14839838233189164938)
XLA Ops:
  0.6 3.2 %prepare.1 = (bf16[16,96,384]{2,1,0:T(8,128)(2,1)}, s32[16]{0:T(128)}, s32[16]{0:T(128)}) custom-call(s32[64]{0:T(128)} %slot_ref.1, s32[128]{0:T(128)} %source_ref.1, s32[128]{0:T(128)} %target_ref.1, bf16[8,96,384]{2,1,0:T(8,128)(2,1)} %amp_hbm.1), custom_call_target="tpu_custom_call" | custom-call | tf_op jit(solution)/shard_map/prepare/pallas_call | solution.py:369
  3.9 55.1 %exchange.1.terms_hbm = bf16[16,96,384]{2,1,0:T(8,128)(2,1)} custom-call(s32[16]{0:T(128)} %get-tuple-element.6.held_ref, f32[4]{0:T(128)} %fock_ref.1, bf16[16,96,384]{2,1,0:T(8,128)(2,1)} %get-tuple-element.7.out_ref, bf16[4,384,384]{2,1,0:T(8,128)(2,1)} %inter_ref.1), custom_call_target="tpu_custom_call" | custom-call | tf_op jit(solution)/shard_map/exchange/pallas_call | solution.py:383
  59.0 4.2 %update.1 = (f32[8,96,384]{2,1,0:T(8,128)}, f32[8,96,384]{2,1,0:T(8,128)}) custom-call(s32[16]{0:T(128)} %get-tuple-element.5.local_ref, f32[8]{0:T(128)} %gap_ref.1, bf16[16,96,384]{2,1,0:T(8,128)(2,1)} %exchange.1.terms_hbm, bf16[8,96,384]{2,1,0:T(8,128)(2,1)} %amp_hbm.1, bf16[8,96,384]{2,1,0:T(8,128)(2,1)} %integrals_hbm.1, f32[8,384]{1,0:T(8,128)} %energy_ref.1), custom_call_target="tpu_custom_call" | custom-call | tf_op jit(solution)/shard_map/update/pallas_call | solution.py:409

commit v4 on v3

--- a/solution.py
+++ b/solution.py
@@ -14,63 +14,21 @@
 SMEM = pltpu.SMEM
 
 
-def prepare_kernel(
-    holders, slot_ref, source_ref, target_ref, amp_ref, out_ref, held_ref, local_ref, first_ref
-):
-    me = lax.axis_index("pairs")
-    pair_count = amp_ref.shape[0]
-    couplings = source_ref.shape[0] // holders
-    base = me * pair_count
-    unroll = 8 if couplings % 8 == 0 else 1
-
-    def holder_step(h, carry):
-        def block(i, ab):
-            first, second = ab
-            for u in range(unroll):
-                local = slot_ref[source_ref[h * couplings + i * unroll + u]] - base
-                mine = (local >= 0) & (local < pair_count)
-                free = first < 0
-                second = jnp.where(mine & jnp.logical_not(free) & (local != first), local, second)
-                first = jnp.where(mine & free, local, first)
-            return first, second
-
-        first, second = lax.fori_loop(
-            0, couplings // unroll, block, (jnp.int32(-1), jnp.int32(-1))
-        )
-        out_ref[h * SRC_CAP] = amp_ref[jnp.maximum(first, 0)]
-        out_ref[h * SRC_CAP + 1] = amp_ref[jnp.maximum(second, 0)]
-        return carry
-
-    lax.fori_loop(0, holders, holder_step, 0)
-
-    def clear(i, carry):
-        first_ref[i] = jnp.int32(-1)
-        return carry
-
-    lax.fori_loop(0, holders, clear, 0)
-
-    def own_step(c, carry):
-        slot = slot_ref[source_ref[me * couplings + c]]
-        owner = lax.div(slot, jnp.int32(pair_count))
-        local = slot - owner * pair_count
-        known = first_ref[owner]
-        first_ref[owner] = jnp.where(known < 0, local, known)
-        rank = jnp.where((known < 0) | (known == local), 0, 1)
-        held_ref[c] = owner * SRC_CAP + rank
-        local_ref[c] = slot_ref[target_ref[me * couplings + c]] - base
-        return carry
-
-    lax.fori_loop(0, couplings, own_step, 0)
-
-
 def exchange_kernel(
     holders,
     quarters,
-    held_ref,
+    slot_ref,
+    source_ref,
+    target_ref,
     fock_ref,
+    amp_ref,
+    inter_hbm,
+    terms_ref,
+    local_ref,
     out_ref,
     inter_ref,
-    terms_ref,
+    held_ref,
+    inter_sem,
     whole,
     picked,
     sent_terms,
@@ -89,7 +47,7 @@
     chunks = len(arrived)
     slots, chunk_rows, width = arrived[0].shape
     rows = chunk_rows * chunks
-    group = inter_ref.shape[0]
+    group = inter_hbm.shape[0]
     half = holders // 2
     my_half = me // half
     in_half = me % half
@@ -107,6 +65,40 @@
         pl.semaphore_signal(
             barrier, inc=1, device_id=(me, (quarter + d) % quarters), device_id_type=MESH
         )
+
+    def inter_copy(c):
+        return pltpu.make_async_copy(inter_hbm.at[c], inter_ref.at[c], inter_sem.at[c])
+
+    def fetch(c, carry):
+        inter_copy(c).start()
+        return carry
+
+    lax.fori_loop(0, group, fetch, 0)
+
+    pair_count = amp_ref.shape[0]
+    couplings = source_ref.shape[0] // holders
+    base = me * pair_count
+    unroll = 8 if couplings % 8 == 0 else 1
+
+    def holder_step(h, carry):
+        def block(i, ab):
+            first, second = ab
+            for u in range(unroll):
+                local = slot_ref[source_ref[h * couplings + i * unroll + u]] - base
+                mine = (local >= 0) & (local < pair_count)
+                free = first < 0
+                second = jnp.where(mine & jnp.logical_not(free) & (local != first), local, second)
+                first = jnp.where(mine & free, local, first)
+            return first, second
+
+        first, second = lax.fori_loop(
+            0, couplings // unroll, block, (jnp.int32(-1), jnp.int32(-1))
+        )
+        out_ref[h * SRC_CAP] = amp_ref[jnp.maximum(first, 0)]
+        out_ref[h * SRC_CAP + 1] = amp_ref[jnp.maximum(second, 0)]
+        return carry
+
+    lax.fori_loop(0, holders, holder_step, 0)
     pl.semaphore_wait(barrier, holders - 1 + quarters - 1)
 
     def owner_copy(k, h):
@@ -153,6 +145,25 @@
         lax.fori_loop(1, half, near, 0)
         own_copy(k).start()
 
+    def own_step(c, carry):
+        slot = slot_ref[source_ref[me * couplings + c]]
+        owner = lax.div(slot, jnp.int32(pair_count))
+
+        def block(i, first):
+            for u in range(unroll):
+                at = couplings - 1 - (i * unroll + u)
+                other = slot_ref[source_ref[me * couplings + at]]
+                same = lax.div(other, jnp.int32(pair_count)) == owner
+                first = jnp.where(same, other, first)
+            return first
+
+        first = lax.fori_loop(0, couplings // unroll, block, slot)
+        held_ref[c] = owner * SRC_CAP + jnp.where(first == slot, 0, 1)
+        local_ref[c] = slot_ref[target_ref[me * couplings + c]] - base
+        return carry
+
+    lax.fori_loop(0, couplings, own_step, 0)
+
     def peer_copy(k, d):
         peer = (quarter + d) % quarters
         return pltpu.make_async_remote_copy(
@@ -236,6 +247,7 @@
         )
 
     def multiply(c, carry):
+        inter_copy(c).wait()
         inter = inter_ref[c]
         left = jnp.dot(inter, whole[c], preferred_element_type=jnp.float32).astype(jnp.bfloat16)
         projected = lax.dot_general(
@@ -366,26 +378,20 @@
     in_smem = pl.BlockSpec(memory_space=SMEM)
     anywhere = pl.BlockSpec(memory_space=pl.ANY)
 
-    outgoing, held, local = pl.pallas_call(
-        functools.partial(prepare_kernel, holders),
+    dma = pltpu.SemaphoreType.DMA
+    terms, local = pl.pallas_call(
+        functools.partial(exchange_kernel, holders, quarters),
         out_shape=(
-            jax.ShapeDtypeStruct((slots, rows, width), bf16),
-            jax.ShapeDtypeStruct((couplings,), jnp.int32),
+            jax.ShapeDtypeStruct((couplings, rows, width), bf16),
             jax.ShapeDtypeStruct((couplings,), jnp.int32),
         ),
-        in_specs=[in_smem, in_smem, in_smem, in_vmem],
-        out_specs=(in_vmem, in_smem, in_smem),
-        scratch_shapes=[SMEM((holders,), jnp.int32)],
-        name="prepare",
-    )(pair_slot, coupling_source, coupling_target, amplitude)
-
-    dma = pltpu.SemaphoreType.DMA
-    terms = pl.pallas_call(
-        functools.partial(exchange_kernel, holders, quarters),
-        out_shape=jax.ShapeDtypeStruct((couplings, rows, width), bf16),
-        in_specs=[in_smem, in_smem, anywhere, in_vmem],
-        out_specs=anywhere,
+        in_specs=[in_smem, in_smem, in_smem, in_smem, in_vmem, anywhere],
+        out_specs=(anywhere, in_smem),
         scratch_shapes=[
+            VMEM((slots, rows, width), bf16),
+            VMEM((group, quarters * rows, width), bf16),
+            SMEM((couplings,), jnp.int32),
+            dma((group,)),
             VMEM((group, quarters * rows, width), bf16),
             VMEM((quarters - 1, chunks, group, chunk_rows, width), bf16),
             VMEM((group, quarters * rows, width), bf16),
@@ -403,7 +409,7 @@
             collective_id=0, has_side_effects=True, vmem_limit_bytes=60 << 20
         ),
         name="exchange",
-    )(held, coupling_fock, outgoing, coupling_intersection)
+    )(pair_slot, coupling_source, coupling_target, coupling_fock, amplitude, coupling_intersection)
 
     out = jax.ShapeDtypeStruct((pair_count, rows, width), jnp.float32)
     return pl.pallas_call(

time: 63.5 us -> 60.4 us (0.951)
  Pallas kernels: 62.6 us -> 59.5 us
    pallas_call x1 -> x0, Pallas kernels: 3.25 us -> none  [per_device(): pl.pallas_call(functools.partial(prepare_kernel, holders), out_shape=(jax...]
where the time goes in v4:
time: 60.4 us; the launch traced here: 60.1 us
  Pallas kernels  59.5 us (99%)
  between operations  0.64 us (1%)
    pallas_call x1, Pallas kernels, per_device(): pl.pallas_call(functools.partial(exchange_kernel, holders, quarters), out...  55.3 us
    pallas_call x1, Pallas kernels, per_device(): pl.pallas_call(update_kernel, out_shape=(out, out), in_specs=[in_smem, in...  4.19 us

profile of v4, /device:TPU:1, one launch (start us, length us, event | category | flops | bytes accessed | tf_op | source)
XLA Modules:
  0.0 60.1 jit_solution(6469563944295748997)
XLA Ops:
  0.6 55.3 %exchange.1 = (bf16[16,96,384]{2,1,0:T(8,128)(2,1)}, s32[16]{0:T(128)}) custom-call(s32[64]{0:T(128)} %slot_ref.1, s32[128]{0:T(128)} %source_ref.1, s32[128]{0:T(128)} %target_ref.1, f32[4]{0:T(128)} %fock_ref.1, bf16[8,96,384]{2,1,0:T(8,128)(2,1)} %amp_hbm.1, bf16[4,384,384]{2,1,0:T(8,128)(2,1)} %inter_hbm.1), custom_call_target="tpu_custom_call" | custom-call | tf_op jit(solution)/shard_map/exchange/pallas_call | solution.py:382
  55.9 4.2 %update.1 = (f32[8,96,384]{2,1,0:T(8,128)}, f32[8,96,384]{2,1,0:T(8,128)}) custom-call(s32[16]{0:T(128)} %get-tuple-element.4.local_ref, f32[8]{0:T(128)} %gap_ref.1, bf16[16,96,384]{2,1,0:T(8,128)(2,1)} %get-tuple-element.5.terms_hbm, bf16[8,96,384]{2,1,0:T(8,128)(2,1)} %amp_hbm.1, bf16[8,96,384]{2,1,0:T(8,128)(2,1)} %integrals_hbm.1, f32[8,384]{1,0:T(8,128)} %energy_ref.1), custom_call_target="tpu_custom_call" | custom-call | tf_op jit(solution)/shard_map/update/pallas_call | solution.py:415

commit v5 on v4

--- a/solution.py
+++ b/solution.py
@@ -40,6 +40,15 @@
     send3,
     recv3,
     local3,
+    inter_x,
+    fock_out,
+    fock_in,
+    half_terms,
+    swap_send,
+    swap_recv,
+    half_send,
+    half_recv,
+    half_local,
     *arrived,
 ):
     me = lax.axis_index("pairs")
@@ -52,6 +61,11 @@
     my_half = me // half
     in_half = me % half
 
+    extra = whole.shape[0] - group
+    full = group - extra
+    partner = (quarter + quarters // 2) % quarters
+    sibling = quarter + 1 - 2 * (quarter % 2)
+
     barrier = pltpu.get_barrier_semaphore()
 
     def greet(j, carry):
@@ -98,8 +112,24 @@
         out_ref[h * SRC_CAP + 1] = amp_ref[jnp.maximum(second, 0)]
         return carry
 
+    fock_out[...] = jnp.full(fock_out.shape, fock_ref[group - 1], jnp.float32)
     lax.fori_loop(0, holders, holder_step, 0)
     pl.semaphore_wait(barrier, holders - 1 + quarters - 1)
+
+    def swaps():
+        for i, (src, dst) in enumerate(((inter_hbm.at[group - 1], inter_x), (fock_out, fock_in))):
+            yield pltpu.make_async_remote_copy(
+                src_ref=src,
+                dst_ref=dst,
+                send_sem=swap_send.at[i],
+                recv_sem=swap_recv.at[i],
+                device_id=(me, partner),
+                device_id_type=MESH,
+            )
+
+    if extra:
+        for copy in swaps():
+            copy.start()
 
     def owner_copy(k, h):
         span = pl.ds(k * chunk_rows, chunk_rows)
@@ -202,6 +232,9 @@
                 return carry
 
             lax.fori_loop(0, group, pick, 0)
+            if extra:
+                last = ((peer + quarters // 2) % quarters) * group + group - 1
+                picked[d - 1, k, group] = arrived[k][held_ref[last]]
 
         for d in range(1, quarters):
             peer_copy(k, d).start()
@@ -212,6 +245,10 @@
             return carry
 
         lax.fori_loop(0, group, keep, 0)
+        if extra:
+            start = pl.multiple_of(quarter * rows + k * chunk_rows, 16)
+            last = partner * group + group - 1
+            whole[group, pl.ds(start, chunk_rows)] = arrived[k][held_ref[last]]
 
     for k in range(chunks):
         for d in range(1, quarters):
@@ -259,7 +296,53 @@
         own_term(c).start()
         return carry
 
-    lax.fori_loop(0, group, multiply, 0)
+    lax.fori_loop(0, full, multiply, 0)
+
+    def half_copy(i):
+        return pltpu.make_async_remote_copy(
+            src_ref=half_terms.at[i, pl.ds(pl.multiple_of((sibling % 2) * rows, 16), rows)],
+            dst_ref=terms_ref.at[(quarter, partner)[i] * group + group - 1],
+            send_sem=half_send.at[i],
+            recv_sem=half_recv.at[i],
+            device_id=(me, sibling),
+            device_id_type=MESH,
+        )
+
+    def half_arrival(i):
+        owner = (sibling, (sibling + quarters // 2) % quarters)[i]
+        return pltpu.make_async_remote_copy(
+            src_ref=half_terms.at[i, pl.ds(pl.multiple_of((sibling % 2) * rows, 16), rows)],
+            dst_ref=terms_ref.at[owner * group + group - 1],
+            send_sem=half_send.at[i],
+            recv_sem=half_recv.at[i],
+            device_id=(me, sibling),
+            device_id_type=MESH,
+        )
+
+    def half_own(i):
+        return pltpu.make_async_copy(
+            half_terms.at[i, pl.ds(pl.multiple_of((quarter % 2) * rows, 16), rows)],
+            terms_ref.at[(quarter, partner)[i] * group + group - 1],
+            half_local.at[i],
+        )
+
+    if extra:
+        inter_copy(group - 1).wait()
+        for copy in swaps():
+            copy.wait_recv()
+        own_half = pl.ds(pl.multiple_of((quarter // 2) * 2 * rows, 16), 2 * rows)
+        for i in range(2):
+            inter_i = inter_x if i else inter_ref.at[group - 1]
+            scale = (fock_in if i else fock_out)[0:1, :]
+            left = jnp.dot(
+                inter_i[own_half, :], whole[group - 1 + i], preferred_element_type=jnp.float32
+            ).astype(jnp.bfloat16)
+            projected = lax.dot_general(
+                left, inter_i[...], (((1,), (1,)), ((), ())), preferred_element_type=jnp.float32
+            )
+            half_terms[i] = (scale * projected).astype(jnp.bfloat16)
+            half_copy(i).start()
+            half_own(i).start()
 
     def finish(c, carry):
         for d in range(1, quarters):
@@ -269,7 +352,14 @@
         own_term(c).wait()
         return carry
 
-    lax.fori_loop(0, group, finish, 0)
+    lax.fori_loop(0, full, finish, 0)
+    if extra:
+        for i in range(2):
+            half_arrival(i).wait_recv()
+            half_copy(i).wait_send()
+            half_own(i).wait()
+        for copy in swaps():
+            copy.wait_send()
     for k in range(chunks):
 
         def sent(j, carry, k=k):
@@ -371,6 +461,7 @@
     couplings = coupling_source.shape[0] // holders
     group = coupling_intersection.shape[0]
     slots = holders * SRC_CAP
+    extra = 1 if quarters == 4 and group > 1 else 0
     chunk_rows = CHUNK_ROWS if rows % CHUNK_ROWS == 0 else rows
     chunks = rows // chunk_rows
     bf16 = jnp.bfloat16
@@ -392,8 +483,8 @@
             VMEM((group, quarters * rows, width), bf16),
             SMEM((couplings,), jnp.int32),
             dma((group,)),
-            VMEM((group, quarters * rows, width), bf16),
-            VMEM((quarters - 1, chunks, group, chunk_rows, width), bf16),
+            VMEM((group + extra, quarters * rows, width), bf16),
+            VMEM((quarters - 1, chunks, group + extra, chunk_rows, width), bf16),
             VMEM((group, quarters * rows, width), bf16),
             dma((chunks, holders)),
             dma((chunks, holders)),
@@ -403,6 +494,15 @@
             dma((group, quarters)),
             dma((group, quarters)),
             dma((group,)),
+            VMEM((quarters * rows, width), bf16),
+            VMEM((8, width), jnp.float32),
+            VMEM((8, width), jnp.float32),
+            VMEM((2, 2 * rows, width), bf16),
+            dma((2,)),
+            dma((2,)),
+            dma((2,)),
+            dma((2,)),
+            dma((2,)),
         ]
         + [VMEM((slots, chunk_rows, width), bf16)] * chunks,
         compiler_params=pltpu.CompilerParams(

time: 60.4 us -> 59.2 us (0.980)
  Pallas kernels: 59.5 us -> 58.3 us
    pallas_call x1, Pallas kernels: 55.3 us -> 54.1 us  [per_device(): pl.pallas_call(functools.partial(exchange_kernel, holders, quarters), out...]
where the time goes in v5:
time: 59.2 us; the launch traced here: 59 us
  Pallas kernels  58.3 us (98%)
  between operations  0.64 us (1%)
    pallas_call x1, Pallas kernels, per_device(): pl.pallas_call(functools.partial(exchange_kernel, holders, quarters), out...  54.1 us
    pallas_call x1, Pallas kernels, per_device(): pl.pallas_call(update_kernel, out_shape=(out, out), in_specs=[in_smem, in...  4.19 us

profile of v5, /device:TPU:1, one launch (start us, length us, event | category | flops | bytes accessed | tf_op | source)
XLA Modules:
  0.0 59.0 jit_solution(4371327553669112222)
XLA Ops:
  0.6 54.1 %exchange.1 = (bf16[16,96,384]{2,1,0:T(8,128)(2,1)}, s32[16]{0:T(128)}) custom-call(s32[64]{0:T(128)} %slot_ref.1, s32[128]{0:T(128)} %source_ref.1, s32[128]{0:T(128)} %target_ref.1, f32[4]{0:T(128)} %fock_ref.1, bf16[8,96,384]{2,1,0:T(8,128)(2,1)} %amp_hbm.1, bf16[4,384,384]{2,1,0:T(8,128)(2,1)} %inter_hbm.1), custom_call_target="tpu_custom_call" | custom-call | tf_op jit(solution)/shard_map/exchange/pallas_call | solution.py:473
  54.8 4.2 %update.1 = (f32[8,96,384]{2,1,0:T(8,128)}, f32[8,96,384]{2,1,0:T(8,128)}) custom-call(s32[16]{0:T(128)} %get-tuple-element.4.local_ref, f32[8]{0:T(128)} %gap_ref.1, bf16[16,96,384]{2,1,0:T(8,128)(2,1)} %get-tuple-element.5.terms_hbm, bf16[8,96,384]{2,1,0:T(8,128)(2,1)} %amp_hbm.1, bf16[8,96,384]{2,1,0:T(8,128)(2,1)} %integrals_hbm.1, f32[8,384]{1,0:T(8,128)} %energy_ref.1), custom_call_target="tpu_custom_call" | custom-call | tf_op jit(solution)/shard_map/update/pallas_call | solution.py:515

commit v6 on v5

--- a/solution.py
+++ b/solution.py
@@ -21,7 +21,7 @@
     source_ref,
     target_ref,
     fock_ref,
-    amp_ref,
+    amp_hbm,
     inter_hbm,
     terms_ref,
     local_ref,
@@ -29,6 +29,8 @@
     inter_ref,
     held_ref,
     inter_sem,
+    amp_ref,
+    amp_sem,
     whole,
     picked,
     sent_terms,
@@ -51,6 +53,8 @@
     half_local,
     *arrived,
 ):
+    amp_copy = pltpu.make_async_copy(amp_hbm, amp_ref, amp_sem)
+    amp_copy.start()
     me = lax.axis_index("pairs")
     quarter = lax.axis_index("dom")
     chunks = len(arrived)
@@ -113,6 +117,7 @@
         return carry
 
     fock_out[...] = jnp.full(fock_out.shape, fock_ref[group - 1], jnp.float32)
+    amp_copy.wait()
     lax.fori_loop(0, holders, holder_step, 0)
     pl.semaphore_wait(barrier, holders - 1 + quarters - 1)
 
@@ -224,7 +229,8 @@
 
         lax.fori_loop(1, holders, take, 0)
         own_copy(k).wait()
-        for d in range(1, quarters):
+        picked_all = []
+        for d in sorted(range(1, quarters), key=lambda d: abs(2 * d - quarters)):
             peer = (quarter + d) % quarters
 
             def pick(c, carry, k=k, d=d, peer=peer):
@@ -235,9 +241,10 @@
             if extra:
                 last = ((peer + quarters // 2) % quarters) * group + group - 1
                 picked[d - 1, k, group] = arrived[k][held_ref[last]]
-
-        for d in range(1, quarters):
-            peer_copy(k, d).start()
+            picked_all.append(d)
+            if len(picked_all) == quarters - 1:
+                for e in picked_all:
+                    peer_copy(k, e).start()
 
         def keep(c, carry, k=k):
             start = pl.multiple_of(quarter * rows + k * chunk_rows, 16)
@@ -413,29 +420,31 @@
         term_copy(c).start()
         return carry
 
-    lax.fori_loop(0, couplings, start_term, 0)
     for p in range(pair_count):
         for copy in in_copies(p):
             copy.start()
+    lax.fori_loop(0, couplings, start_term, 0)
     columns[...] = jnp.transpose(energy_ref[...])
-    residual[...] = jnp.zeros_like(residual)
-
-    def add_term(c, carry):
-        term_copy(c).wait()
-        p = local_ref[c]
-        residual[p] = residual[p] + terms[c].astype(jnp.float32)
-        return carry
-
-    lax.fori_loop(0, couplings, add_term, 0)
     own_rows = columns[pl.ds(pl.multiple_of(quarter * rows, 8), rows), :]
+
+    def denominator(p):
+        return own_rows[:, p : p + 1] + energy_ref[p : p + 1, :] + gap_ref[p]
+
     for p in range(pair_count):
         for copy in in_copies(p):
             copy.wait()
         current = amp[p].astype(jnp.float32)
-        denominator = own_rows[:, p : p + 1] + energy_ref[p : p + 1, :] + gap_ref[p]
-        rest = integrals[p].astype(jnp.float32) + denominator * current - residual[p]
-        residual[p] = rest
-        new[p] = current - rest / denominator
+        residual[p] = integrals[p].astype(jnp.float32) + denominator(p) * current
+
+    def add_term(c, carry):
+        term_copy(c).wait()
+        p = local_ref[c]
+        residual[p] = residual[p] - terms[c].astype(jnp.float32)
+        return carry
+
+    lax.fori_loop(0, couplings, add_term, 0)
+    for p in range(pair_count):
+        new[p] = amp[p].astype(jnp.float32) - residual[p] / denominator(p)
         for copy in out_copies(p):
             copy.start()
     for p in range(pair_count):
@@ -476,13 +485,15 @@
             jax.ShapeDtypeStruct((couplings, rows, width), bf16),
             jax.ShapeDtypeStruct((couplings,), jnp.int32),
         ),
-        in_specs=[in_smem, in_smem, in_smem, in_smem, in_vmem, anywhere],
+        in_specs=[in_smem, in_smem, in_smem, in_smem, anywhere, anywhere],
         out_specs=(anywhere, in_smem),
         scratch_shapes=[
             VMEM((slots, rows, width), bf16),
             VMEM((group, quarters * rows, width), bf16),
             SMEM((couplings,), jnp.int32),
             dma((group,)),
+            VMEM((pair_count, rows, width), bf16),
+            dma(()),
             VMEM((group + extra, quarters * rows, width), bf16),
             VMEM((quarters - 1, chunks, group + extra, chunk_rows, width), bf16),
             VMEM((group, quarters * rows, width), bf16),

time: 59.2 us -> 59 us (level)
  no operation moved by 1% of the time
where the time goes in v6:
time: 59 us; the launch traced here: 58.8 us
  Pallas kernels  58.2 us (99%)
  between operations  0.64 us (1%)
    pallas_call x1, Pallas kernels, per_device(): pl.pallas_call(functools.partial(exchange_kernel, holders, quarters), out...  53.6 us
    pallas_call x1, Pallas kernels, per_device(): pl.pallas_call(update_kernel, out_shape=(out, out), in_specs=[in_smem, in...  4.55 us

profile of v6, /device:TPU:1, one launch (start us, length us, event | category | flops | bytes accessed | tf_op | source)
XLA Modules:
  0.0 58.8 jit_solution(530336316561434263)
XLA Ops:
  0.6 53.6 %exchange.1 = (bf16[16,96,384]{2,1,0:T(8,128)(2,1)}, s32[16]{0:T(128)}) custom-call(s32[64]{0:T(128)} %slot_ref.1, s32[128]{0:T(128)} %source_ref.1, s32[128]{0:T(128)} %target_ref.1, f32[4]{0:T(128)} %fock_ref.1, bf16[8,96,384]{2,1,0:T(8,128)(2,1)} %amp_hbm.3, bf16[4,384,384]{2,1,0:T(8,128)(2,1)} %inter_hbm.1), custom_call_target="tpu_custom_call" | custom-call | tf_op jit(solution)/shard_map/exchange/pallas_call | solution.py:482
  54.2 4.6 %update.1 = (f32[8,96,384]{2,1,0:T(8,128)}, f32[8,96,384]{2,1,0:T(8,128)}) custom-call(s32[16]{0:T(128)} %get-tuple-element.4.local_ref, f32[8]{0:T(128)} %gap_ref.1, bf16[16,96,384]{2,1,0:T(8,128)(2,1)} %get-tuple-element.5.terms_hbm, bf16[8,96,384]{2,1,0:T(8,128)(2,1)} %amp_hbm.3, bf16[8,96,384]{2,1,0:T(8,128)(2,1)} %integrals_hbm.1, f32[8,384]{1,0:T(8,128)} %energy_ref.1), custom_call_target="tpu_custom_call" | custom-call | tf_op jit(solution)/shard_map/update/pallas_call | solution.py:526

commit v7 on v6

--- a/solution.py
+++ b/solution.py
@@ -8,7 +8,7 @@
 from jax.sharding import PartitionSpec as P
 
 SRC_CAP = 2
-CHUNK_ROWS = 16
+CHUNK_ROWS = 32
 MESH = pl.DeviceIdType.MESH
 VMEM = pltpu.VMEM
 SMEM = pltpu.SMEM

time: 59 us -> 59.4 us (level)
  no operation moved by 1% of the time
where the time goes in v7:
time: 59.4 us; the launch traced here: 59.1 us
  Pallas kernels  58.5 us (98%)
  between operations  0.64 us (1%)
    pallas_call x1, Pallas kernels, per_device(): pl.pallas_call(functools.partial(exchange_kernel, holders, quarters), out...  53.9 us
    pallas_call x1, Pallas kernels, per_device(): pl.pallas_call(update_kernel, out_shape=(out, out), in_specs=[in_smem, in...  4.55 us

profile of v7, /device:TPU:1, one launch (start us, length us, event | category | flops | bytes accessed | tf_op | source)
XLA Modules:
  0.0 59.1 jit_solution(13254511465858090735)
XLA Ops:
  0.6 53.9 %exchange.1 = (bf16[16,96,384]{2,1,0:T(8,128)(2,1)}, s32[16]{0:T(128)}) custom-call(s32[64]{0:T(128)} %slot_ref.1, s32[128]{0:T(128)} %source_ref.1, s32[128]{0:T(128)} %target_ref.1, f32[4]{0:T(128)} %fock_ref.1, bf16[8,96,384]{2,1,0:T(8,128)(2,1)} %amp_hbm.3, bf16[4,384,384]{2,1,0:T(8,128)(2,1)} %inter_hbm.1), custom_call_target="tpu_custom_call" | custom-call | tf_op jit(solution)/shard_map/exchange/pallas_call | solution.py:482
  54.6 4.6 %update.1 = (f32[8,96,384]{2,1,0:T(8,128)}, f32[8,96,384]{2,1,0:T(8,128)}) custom-call(s32[16]{0:T(128)} %get-tuple-element.4.local_ref, f32[8]{0:T(128)} %gap_ref.1, bf16[16,96,384]{2,1,0:T(8,128)(2,1)} %get-tuple-element.5.terms_hbm, bf16[8,96,384]{2,1,0:T(8,128)(2,1)} %amp_hbm.3, bf16[8,96,384]{2,1,0:T(8,128)(2,1)} %integrals_hbm.1, f32[8,384]{1,0:T(8,128)} %energy_ref.1), custom_call_target="tpu_custom_call" | custom-call | tf_op jit(solution)/shard_map/update/pallas_call | solution.py:526
